TPU v7x, 512 devices: a whole 4x8x8 slice. The times are simulated.
512 devices in a mesh: gx: 16 (over z, x_lo), gy: 32 (over x_hi, y, core).
Axes of the slice: x: 4 (x_hi: 2, x_lo: 2; x = x_hi * 2 + x_lo), y: 8, z: 8, core: 2. Of those that a mesh axis runs over, the one named last changes fastest.
Arguments:
- features: bfloat16 [16, 32, 1600, 128], P('gx', 'gy'), may hold values from -6 to 6
- cotangent: bfloat16 [16, 32, 1600, 128], P('gx', 'gy'), may hold values from -6 to 6
- w_order0: bfloat16 [320, 320], replicated, may hold values from -0.3125 to 0.3125
- w_order1: bfloat16 [2, 256, 256], replicated, may hold values from -0.375 to 0.375
- w_order2: bfloat16 [2, 192, 192], replicated, may hold values from -0.4375 to 0.4375
- w_order3: bfloat16 [2, 128, 128], replicated, may hold values from -0.5 to 0.5
- w_order4: bfloat16 [2, 64, 64], replicated, may hold values from -0.75 to 0.75
- to_grid: float32 [100, 25], replicated, may hold values from -1.25 to 1.25
- from_grid: float32 [25, 100], replicated, may hold values from -0.625 to 0.625
- edge_harmonics: float32 [16, 32, 25, 256], P('gx', 'gy'), may hold values from -5 to 5
- edge_source: int32 [16, 32, 256], P('gx', 'gy'), may hold values from 0 to 383, as said below
- edge_target: int32 [16, 32, 256], P('gx', 'gy'), may hold values from 0 to 128, as said below
- send_list: int32 [16, 32, 8, 32], P('gx', 'gy'), may hold values from 0 to 127, as said below
Outputs:
- layer_out: bfloat16 [16, 32, 1600, 128], P('gx', 'gy')
- feature_grad: float32 [16, 32, 1600, 128], P('gx', 'gy')
Inputs may be any that keep to these rules, and one draw needn't show every extreme that they name: `edge_source`: on each cell the live edges come first and padding follows; the number of live edges of a cell is at least 128, and all 256 slots are live on some cell in every draw. Columns below 128 are owned atoms, column 128 + d * 32 + i is entry i of ghost block d. `edge_target`: the value 128 marks a padded edge slot, exactly those slots after a cell's live edges. `send_list`: the 32 entries of one cell and one direction are distinct.
All inputs are finite; a program needn't handle non-finite values.
Results may differ from a plain program's by a relative error of at most 0.0034.
Values may be sent and summed in bfloat16 or wider, within the bound.
A program may use at most 64 MiB of HBM per device.

v0:
```python
import functools

import jax
import jax.numpy as jnp
from jax import lax
from jax.experimental import pallas as pl
from jax.experimental.pallas import tpu as pltpu
from jax.sharding import PartitionSpec as P

DIRECTIONS = ((-1, -1), (-1, 0), (-1, 1), (0, -1), (0, 1), (1, -1), (1, 0), (1, 1))
EDGE_NORM = 0.35
MESH = pl.DeviceIdType.MESH
F32 = jnp.float32
BF16 = jnp.bfloat16

COEFS = 25
CH = 64
GRID = 100
ATOMS = 128
EDGES = 256
GHOST = 32
ROWS = COEFS * CH
GHOSTS = 8 * GHOST
SPANS = ((0, 320, 384), (320, 512, 512), (832, 384, 384), (1216, 256, 256), (1472, 128, 128))
ORDER = (1, 2, 0, 3, 4)
SEND_DIRS = (0, 2, 5, 7, 1, 6, 3, 4)


def nn(left, right):
    return jnp.dot(left, right, preferred_element_type=F32)


def nt(left, right):
    return lax.dot_general(left, right, (((1,), (1,)), ((), ())), preferred_element_type=F32)


def parts(value, count):
    pieces = []
    for _ in range(count - 1):
        piece = value.astype(BF16)
        pieces.append(piece)
        value = value - piece.astype(F32)
    pieces.append(value.astype(BF16))
    return pieces


def iota(shape, dim):
    return lax.broadcasted_iota(jnp.int32, shape, dim)


def ones_where(mask):
    return jnp.where(mask, 1.0, 0.0).astype(F32)


def identity(size):
    return ones_where(iota((size, size), 0) == iota((size, size), 1)).astype(BF16)


def kernel(
    count_x,
    count_y,
    feat_hbm,
    cot_hbm,
    w0_hbm,
    w1_hbm,
    w2_hbm,
    w3_hbm,
    w4_hbm,
    tg_hbm,
    fg_hbm,
    harm_hbm,
    source_ref,
    target_ref,
    list_ref,
    layer_ref,
    grad_ref,
    feat,
    cot,
    w0,
    w1,
    w2,
    w3,
    w4,
    tg,
    fg,
    harm,
    feat32,
    cot32,
    out0,
    out1,
    out2,
    out3,
    out4,
    in0,
    in1,
    in2,
    in3,
    in4,
    back0,
    back1,
    back2,
    back3,
    back4,
    home0,
    home1,
    home2,
    home3,
    home4,
    mix1,
    mix2,
    mix3,
    mix4,
    harm_t,
    pick_list,
    pick_source,
    pick_source_t,
    pick_target,
    pick_target_t,
    kron_a,
    kron_at,
    kron_b,
    kron_bt,
    grid_feat,
    d_product,
    product,
    d_feat,
    agg,
    d_agg,
    own_t,
    local_sem,
    out_sem,
    in_sem,
    back_sem,
    home_sem,
):
    outs = (out0, out1, out2, out3, out4)
    ins = (in0, in1, in2, in3, in4)
    backs = (back0, back1, back2, back3, back4)
    homes = (home0, home1, home2, home3, home4)
    mixes = (w0, mix1, mix2, mix3, mix4)

    at_x = lax.axis_index("gx")
    at_y = lax.axis_index("gy")

    def cell(index, sign):
        step_x, step_y = DIRECTIONS[index]
        return (
            lax.rem(at_x + (sign * step_x + count_x), count_x),
            lax.rem(at_y + (sign * step_y + count_y), count_y),
        )

    loads = [
        pltpu.make_async_copy(source, target, local_sem.at[number])
        for number, (source, target) in enumerate(
            (
                (feat_hbm, feat),
                (harm_hbm, harm),
                (tg_hbm, tg),
                (fg_hbm, fg),
                (cot_hbm, cot),
                (w0_hbm, w0),
                (w1_hbm, w1),
                (w2_hbm, w2),
                (w3_hbm, w3),
                (w4_hbm, w4),
            )
        )
    ]
    for load in loads:
        load.start()

    barrier = pltpu.get_barrier_semaphore()
    for index in range(8):
        pl.semaphore_signal(barrier, inc=1, device_id=cell(index, 1), device_id_type=MESH)

    list_row = nn(
        list_ref[...].astype(F32).astype(BF16),
        ones_where(iota((GHOST, GHOSTS), 0) == (iota((GHOST, GHOSTS), 1) & 31)).astype(BF16),
    )
    list_row = jnp.where(iota((8, GHOSTS), 0) == (iota((8, GHOSTS), 1) >> 5), list_row, 0.0)
    list_row = jnp.sum(list_row, axis=0, keepdims=True)
    pick_list[...] = ones_where(iota((ATOMS, GHOSTS), 0).astype(F32) == list_row).astype(BF16)
    eye = identity(256)
    pick_list_t = nt(eye, pick_list[...]).astype(BF16)

    loads[0].wait()

    lending = {}
    returning = {}
    started = False
    for order in ORDER:
        first, rows, lanes = SPANS[order]
        lent = nt(pick_list_t, feat[first : first + rows, :]).astype(BF16)
        outs[order][:, :, 0:rows] = lent.reshape(8, GHOST, rows)
        if not started:
            pl.semaphore_wait(barrier, 8)
            started = True
        for index in SEND_DIRS:
            copy = pltpu.make_async_remote_copy(
                src_ref=outs[order].at[index],
                dst_ref=ins[order].at[index],
                send_sem=out_sem.at[order, index],
                recv_sem=in_sem.at[order, index],
                device_id=cell(index, -1),
                device_id_type=MESH,
            )
            copy.start()
            lending[order, index] = copy

    pick_source[...] = ones_where(
        iota((ATOMS + GHOSTS, EDGES), 0) == source_ref[...]
    ).astype(BF16)
    pick_target[...] = ones_where(iota((ATOMS, EDGES), 0) == target_ref[...]).astype(BF16)
    pick_source_t[...] = nt(eye, pick_source[...]).astype(BF16)
    pick_target_t[...] = nt(eye, pick_target[...]).astype(BF16)

    loads[1].wait()
    harm_parts = [nt(eye, piece).astype(BF16) for piece in parts(harm[...], 3)]
    for order in ORDER:
        first, rows, lanes = SPANS[order]
        spread = ones_where(
            ((iota((COEFS, rows), 1) + first) >> 6) == iota((COEFS, rows), 0)
        ).astype(BF16)
        wide = nn(harm_parts[0], spread) + nn(harm_parts[1], spread) + nn(harm_parts[2], spread)
        harm_t[:, first : first + rows] = wide

    loads[2].wait()
    loads[3].wait()
    grid_rows = ones_where((iota((GRID * 8, GRID), 0) >> 3) == iota((GRID * 8, GRID), 1)).astype(BF16)
    grid_cols = ones_where((iota((GRID, GRID * 8), 1) >> 3) == iota((GRID, GRID * 8), 0)).astype(BF16)
    coef_rows = ones_where((iota((COEFS * 8, COEFS), 0) >> 3) == iota((COEFS * 8, COEFS), 1)).astype(BF16)
    coef_cols = ones_where((iota((COEFS, COEFS * 8), 1) >> 3) == iota((COEFS, COEFS * 8), 0)).astype(BF16)
    tall = (iota((GRID * 8, COEFS * 8), 0) & 7) == (iota((GRID * 8, COEFS * 8), 1) & 7)
    flat = (iota((COEFS * 8, GRID * 8), 0) & 7) == (iota((COEFS * 8, GRID * 8), 1) & 7)
    for number, (to_part, from_part) in enumerate(zip(parts(tg[...], 2), parts(fg[...], 2))):
        kron_a[number] = jnp.where(
            tall, nn(nn(grid_rows, to_part).astype(BF16), coef_cols), 0.0
        ).astype(BF16)
        kron_at[number] = jnp.where(
            flat, nn(nt(coef_rows, to_part).astype(BF16), grid_cols), 0.0
        ).astype(BF16)
        kron_b[number] = jnp.where(
            flat, nn(nn(coef_rows, from_part).astype(BF16), grid_cols), 0.0
        ).astype(BF16)
        kron_bt[number] = jnp.where(
            tall, nn(nt(grid_rows, from_part).astype(BF16), coef_cols), 0.0
        ).astype(BF16)

    feat32[...] = feat[...].astype(F32).reshape(COEFS, 8, 8, ATOMS)
    loads[4].wait()
    cot32[...] = cot[...].astype(F32).reshape(COEFS, 8, 8, ATOMS)

    def pair(ref, at):
        return jnp.concatenate(
            [ref[:, 2 * at + side].reshape(COEFS * 8, ATOMS) for side in range(2)], axis=1
        )

    def unpair(ref, at, value):
        for side in range(2):
            ref[:, 2 * at + side] = value[:, side * ATOMS : (side + 1) * ATOMS].reshape(
                COEFS, 8, ATOMS
            )

    def times(kron, value):
        high, low = parts(value, 2)
        return nn(kron[0], high) + nn(kron[1], high) + nn(kron[0], low)

    @pl.loop(0, 4)
    def _(at):
        feat_pair = pair(feat32, at).astype(BF16)
        grid_feat[at] = nn(kron_a[0], feat_pair) + nn(kron_a[1], feat_pair)
        cot_pair = pair(cot32, at).astype(BF16)
        d_product[at] = nn(kron_bt[0], cot_pair) + nn(kron_bt[1], cot_pair)

    for number in range(5, 10):
        loads[number].wait()
    for weight, mix in ((w1, mix1), (w2, mix2), (w3, mix3), (w4, mix4)):
        size = weight.shape[1]
        left = ones_where(iota((size, 2 * size), 0) == iota((size, 2 * size), 1)).astype(BF16)
        right = ones_where(iota((size, 2 * size), 0) + size == iota((size, 2 * size), 1)).astype(BF16)
        mix[0:size, :] = (nn(weight[0], left) - nn(weight[1], right)).astype(BF16)
        mix[size : 2 * size, :] = (nn(weight[1], left) + nn(weight[0], right)).astype(BF16)

    for order in ORDER:
        first, rows, lanes = SPANS[order]
        columns = nt(pick_source_t[:, 0:ATOMS], feat[first : first + rows, :])
        for index in SEND_DIRS:
            lending[order, index].wait_recv()
        ghosts = ins[order][...].reshape(GHOSTS, lanes)[:, 0:rows]
        columns = columns + nn(pick_source_t[:, ATOMS:], ghosts)
        filtered = (columns * harm_t[:, first : first + rows]).astype(BF16)
        message = nt(mixes[order][...], filtered)
        high, low = parts(message, 2)
        total = nt(high, pick_target[...]) + nt(low, pick_target[...])
        agg[first // CH : (first + rows) // CH] = (total * EDGE_NORM).reshape(
            rows // CH, 8, 8, ATOMS
        )

    @pl.loop(0, 4)
    def _(at):
        grid_agg = times(kron_a, pair(agg, at))
        gate = jax.nn.sigmoid(grid_agg)
        active = grid_agg * gate
        slope = gate * (1.0 + grid_agg * (1.0 - gate))
        feat_at = grid_feat[at]
        d_at = d_product[at]
        product[at] = active * feat_at
        d_feat[at] = d_at * active
        unpair(d_agg, at, times(kron_at, d_at * feat_at * slope) * EDGE_NORM)

    for order in ORDER:
        first, rows, lanes = SPANS[order]
        d_rows = d_agg[first // CH : (first + rows) // CH].reshape(rows, ATOMS).astype(BF16)
        d_message = nt(pick_target_t[...], d_rows).astype(BF16)
        d_filtered = nn(d_message, mixes[order][...])
        high, low = parts(d_filtered * harm_t[:, first : first + rows], 2)
        ghosts = nn(pick_source[ATOMS:, :], high) + nn(pick_source[ATOMS:, :], low)
        backs[order][:, :, 0:rows] = ghosts.astype(BF16).reshape(8, GHOST, rows)
        for index in SEND_DIRS:
            copy = pltpu.make_async_remote_copy(
                src_ref=backs[order].at[index],
                dst_ref=homes[order].at[index],
                send_sem=back_sem.at[order, index],
                recv_sem=home_sem.at[order, index],
                device_id=cell(index, 1),
                device_id_type=MESH,
            )
            copy.start()
            returning[order, index] = copy
        own_t[:, first : first + rows] = nn(pick_source[0:ATOMS, :], high) + nn(
            pick_source[0:ATOMS, :], low
        )

    @pl.loop(0, 4)
    def _(at):
        unpair(feat32, at, pair(feat32, at) + times(kron_b, product[at]))
        unpair(cot32, at, pair(cot32, at) + times(kron_at, d_feat[at]))

    layer_ref[...] = feat32[...].reshape(ROWS, ATOMS).astype(BF16)

    for order in ORDER:
        first, rows, lanes = SPANS[order]
        for index in SEND_DIRS:
            returning[order, index].wait_recv()
        arrived = homes[order][...].reshape(GHOSTS, lanes)[:, 0:rows]
        total = own_t[:, first : first + rows] + nn(pick_list[...], arrived)
        node = cot32[first // CH : (first + rows) // CH].reshape(rows, ATOMS)
        grad_ref[first : first + rows, :] = node + jnp.transpose(total)

    for copy in (*lending.values(), *returning.values()):
        copy.wait_send()


def per_device(
    features,
    cotangent,
    w_order0,
    w_order1,
    w_order2,
    w_order3,
    w_order4,
    to_grid,
    from_grid,
    edge_harmonics,
    edge_source,
    edge_target,
    send_list,
):
    count_x = lax.axis_size("gx")
    count_y = lax.axis_size("gy")
    in_hbm = pl.BlockSpec(memory_space=pl.ANY)
    in_vmem = pl.BlockSpec(memory_space=pltpu.VMEM)
    grids = pltpu.VMEM((4, GRID * 8, 2 * ATOMS), F32)
    tiles = pltpu.VMEM((COEFS, 8, 8, ATOMS), F32)
    tall = pltpu.VMEM((2, GRID * 8, COEFS * 8), BF16)
    flat = pltpu.VMEM((2, COEFS * 8, GRID * 8), BF16)
    blocks = [pltpu.VMEM((8, GHOST, lanes), BF16) for _, _, lanes in SPANS]
    copies = pltpu.SemaphoreType.DMA((5, 8))
    layer, grad = pl.pallas_call(
        functools.partial(kernel, count_x, count_y),
        out_shape=(
            jax.ShapeDtypeStruct((ROWS, ATOMS), BF16),
            jax.ShapeDtypeStruct((ROWS, ATOMS), F32),
        ),
        in_specs=[in_hbm] * 10 + [in_vmem] * 3,
        out_specs=(in_vmem, in_vmem),
        scratch_shapes=[
            pltpu.VMEM((ROWS, ATOMS), BF16),
            pltpu.VMEM((ROWS, ATOMS), BF16),
            pltpu.VMEM(w_order0.shape, BF16),
            pltpu.VMEM(w_order1.shape, BF16),
            pltpu.VMEM(w_order2.shape, BF16),
            pltpu.VMEM(w_order3.shape, BF16),
            pltpu.VMEM(w_order4.shape, BF16),
            pltpu.VMEM((GRID, COEFS), F32),
            pltpu.VMEM((COEFS, GRID), F32),
            pltpu.VMEM((COEFS, EDGES), F32),
            tiles,
            tiles,
            *blocks,
            *blocks,
            *blocks,
            *blocks,
            *[pltpu.VMEM((rows, rows), BF16) for _, rows, _ in SPANS[1:]],
            pltpu.VMEM((EDGES, ROWS), F32),
            pltpu.VMEM((ATOMS, GHOSTS), BF16),
            pltpu.VMEM((ATOMS + GHOSTS, EDGES), BF16),
            pltpu.VMEM((EDGES, ATOMS + GHOSTS), BF16),
            pltpu.VMEM((ATOMS, EDGES), BF16),
            pltpu.VMEM((EDGES, ATOMS), BF16),
            tall,
            flat,
            flat,
            tall,
            grids,
            grids,
            grids,
            grids,
            tiles,
            tiles,
            pltpu.VMEM((ATOMS, ROWS), F32),
            pltpu.SemaphoreType.DMA((10,)),
            copies,
            copies,
            copies,
            copies,
        ],
        compiler_params=pltpu.CompilerParams(
            collective_id=0, has_side_effects=True, vmem_limit_bytes=56 * 1024 * 1024
        ),
        name="layer",
    )(
        features[0, 0],
        cotangent[0, 0],
        w_order0,
        w_order1,
        w_order2,
        w_order3,
        w_order4,
        to_grid,
        from_grid,
        edge_harmonics[0, 0],
        edge_source[0],
        edge_target[0],
        send_list[0, 0],
    )
    return layer[None, None], grad[None, None]


def solution(mesh):
    cells = P("gx", "gy", None, None)
    placed = (cells, cells, P(), P(), P(), P(), P(), P(), P(), cells, P("gx", "gy", None), P("gx", "gy", None), cells)
    return jax.shard_map(
        per_device,
        mesh=mesh,
        in_specs=placed,
        out_specs=(cells, cells),
        check_vma=False,
    )
```

profile of v0, /device:TPU:1, one launch (start us, length us, event | category | flops | bytes accessed | tf_op | source)
XLA Modules:
  0.0 54.2 jit_solution(8543663485891467018)
XLA Ops:
  0.6 0.0 copy-start.1
  0.6 1.4 %copy.18 = f32[1,1,25,256]{3,2,1,0:T(8,128)} copy(f32[1,1,25,256]{3,1,2,0:T(1,128)} %param.22) | data formatting | bytes 51200
  2.0 0.0 copy-done.1
  2.0 0.7 %copy.15.tg_hbm = f32[100,25]{1,0:T(8,128)} copy(f32[100,25]{0,1:T(8,128)S(1)} %copy-done.1) | data formatting | bytes 20000 | tf_op args[7]
  2.7 48.7 %layer.1 = (bf16[1600,128]{1,0:T(8,128)(2,1)}, f32[1600,128]{1,0:T(8,128)}) custom-call(bf16[1600,128]{1,0:T(8,128)(2,1)} %bitcast.12, bf16[1600,128]{1,0:T(8,128)(2,1)} %bitcast.13, bf16[320,320]{1,0:T(8,128)(2,1)} %w0_hbm.1, bf16[2,256,256]{2,1,0:T(8,128)(2,1)} %w1_hbm.1, bf16[2,192,192]{2,1,0:T(8,128)(2,1)} %w2_hbm.1, bf16[2,128,128]{2,1,0:T(8,128)(2,1)} %w3_hbm.1, ...), custom_call_target="tpu_custom_call" | custom-call | tf_op jit(solution)/shard_map/layer/pallas_call | solution.py:379
  51.4 0.0 copy-start
  51.4 1.9 %copy.21 = bf16[1,1,1600,128]{3,2,1,0:T(8,128)(2,1)} copy(bf16[1,1,1600,128]{3,2,1,0:T(8,128)(2,1)} %bitcast.11) | data formatting | bytes 819200
  53.3 0.0 copy-done
  53.3 0.9 %copy.22 = f32[1,1,1600,128]{3,2,1,0:T(8,128)} copy(f32[1,1,1600,128]{3,2,1,0:T(8,128)S(1)} %bitcast.10) | data formatting | bytes 1638400
Async XLA Ops:
  0.6 1.4 %copy-start.1 = (f32[100,25]{0,1:T(8,128)S(1)}, f32[100,25]{0,1:T(8,128)}, u32[]{:S(2)}) copy-start(f32[100,25]{0,1:T(8,128)} %param.20) | copy-start | bytes 30004
  51.4 1.9 %copy-start = (f32[1600,128]{1,0:T(8,128)S(1)}, f32[1600,128]{1,0:T(8,128)}, u32[]{:S(2)}) copy-start(f32[1600,128]{1,0:T(8,128)} %get-tuple-element.5) | copy-start | bytes 2457604
where the time goes:
time: 54.4 us; the launch traced here: 54.2 us
  Pallas kernels  48.7 us (90%)
  local copies, waits for them, and re-layouts  4.84 us (9%)
  between operations  0.66 us (1%)
    pallas_call x1, Pallas kernels, per_device(): pl.pallas_call(functools.partial(kernel, count_x, count_y), out_shape=(ja...  48.7 us
    unnamed x8, local copies, waits for them, and re-layouts  4.84 us

commit v1 on v0

--- a/solution.py
+++ b/solution.py
@@ -22,7 +22,9 @@
 ROWS = COEFS * CH
 GHOSTS = 8 * GHOST
 SPANS = ((0, 320, 384), (320, 512, 512), (832, 384, 384), (1216, 256, 256), (1472, 128, 128))
-ORDER = (1, 2, 0, 3, 4)
+ORDER = (3, 0, 1, 2, 4)
+BACK_ORDER = (4, 0, 1, 2, 3)
+STRIPES = ((0, 256), (256, 256), (512, 256), (768, 32))
 SEND_DIRS = (0, 2, 5, 7, 1, 6, 3, 4)
 
 
@@ -69,9 +71,9 @@
     tg_hbm,
     fg_hbm,
     harm_hbm,
-    source_ref,
-    target_ref,
-    list_ref,
+    source_hbm,
+    target_hbm,
+    list_hbm,
     layer_ref,
     grad_ref,
     feat,
@@ -84,6 +86,9 @@
     tg,
     fg,
     harm,
+    source_ref,
+    target_ref,
+    list_ref,
     feat32,
     cot32,
     out0,
@@ -122,8 +127,8 @@
     kron_bt,
     grid_feat,
     d_product,
-    product,
-    d_feat,
+    grid_agg,
+    joint,
     agg,
     d_agg,
     own_t,
@@ -153,8 +158,11 @@
         pltpu.make_async_copy(source, target, local_sem.at[number])
         for number, (source, target) in enumerate(
             (
+                (list_hbm, list_ref),
                 (feat_hbm, feat),
-                (harm_hbm, harm),
+                (source_hbm, source_ref),
+                (target_hbm, target_ref),
+                (harm_hbm.at[:, 0], harm),
                 (tg_hbm, tg),
                 (fg_hbm, fg),
                 (cot_hbm, cot),
@@ -173,6 +181,7 @@
     for index in range(8):
         pl.semaphore_signal(barrier, inc=1, device_id=cell(index, 1), device_id_type=MESH)
 
+    loads[0].wait()
     list_row = nn(
         list_ref[...].astype(F32).astype(BF16),
         ones_where(iota((GHOST, GHOSTS), 0) == (iota((GHOST, GHOSTS), 1) & 31)).astype(BF16),
@@ -183,7 +192,7 @@
     eye = identity(256)
     pick_list_t = nt(eye, pick_list[...]).astype(BF16)
 
-    loads[0].wait()
+    loads[1].wait()
 
     lending = {}
     returning = {}
@@ -207,6 +216,8 @@
             copy.start()
             lending[order, index] = copy
 
+    loads[2].wait()
+    loads[3].wait()
     pick_source[...] = ones_where(
         iota((ATOMS + GHOSTS, EDGES), 0) == source_ref[...]
     ).astype(BF16)
@@ -214,7 +225,7 @@
     pick_source_t[...] = nt(eye, pick_source[...]).astype(BF16)
     pick_target_t[...] = nt(eye, pick_target[...]).astype(BF16)
 
-    loads[1].wait()
+    loads[4].wait()
     harm_parts = [nt(eye, piece).astype(BF16) for piece in parts(harm[...], 3)]
     for order in ORDER:
         first, rows, lanes = SPANS[order]
@@ -224,8 +235,8 @@
         wide = nn(harm_parts[0], spread) + nn(harm_parts[1], spread) + nn(harm_parts[2], spread)
         harm_t[:, first : first + rows] = wide
 
-    loads[2].wait()
-    loads[3].wait()
+    loads[5].wait()
+    loads[6].wait()
     grid_rows = ones_where((iota((GRID * 8, GRID), 0) >> 3) == iota((GRID * 8, GRID), 1)).astype(BF16)
     grid_cols = ones_where((iota((GRID, GRID * 8), 1) >> 3) == iota((GRID, GRID * 8), 0)).astype(BF16)
     coef_rows = ones_where((iota((COEFS * 8, COEFS), 0) >> 3) == iota((COEFS * 8, COEFS), 1)).astype(BF16)
@@ -234,10 +245,10 @@
     flat = (iota((COEFS * 8, GRID * 8), 0) & 7) == (iota((COEFS * 8, GRID * 8), 1) & 7)
     for number, (to_part, from_part) in enumerate(zip(parts(tg[...], 2), parts(fg[...], 2))):
         kron_a[number] = jnp.where(
-            tall, nn(nn(grid_rows, to_part).astype(BF16), coef_cols), 0.0
+            tall, nn(nt(grid_rows, to_part).astype(BF16), coef_cols), 0.0
         ).astype(BF16)
         kron_at[number] = jnp.where(
-            flat, nn(nt(coef_rows, to_part).astype(BF16), grid_cols), 0.0
+            flat, nn(nn(coef_rows, to_part).astype(BF16), grid_cols), 0.0
         ).astype(BF16)
         kron_b[number] = jnp.where(
             flat, nn(nn(coef_rows, from_part).astype(BF16), grid_cols), 0.0
@@ -247,7 +258,7 @@
         ).astype(BF16)
 
     feat32[...] = feat[...].astype(F32).reshape(COEFS, 8, 8, ATOMS)
-    loads[4].wait()
+    loads[7].wait()
     cot32[...] = cot[...].astype(F32).reshape(COEFS, 8, 8, ATOMS)
 
     def pair(ref, at):
@@ -261,9 +272,11 @@
                 COEFS, 8, ATOMS
             )
 
-    def times(kron, value):
+    def times(kron, value, stripe):
         high, low = parts(value, 2)
-        return nn(kron[0], high) + nn(kron[1], high) + nn(kron[0], low)
+        return (
+            nn(kron[0, :, stripe], high) + nn(kron[1, :, stripe], high) + nn(kron[0, :, stripe], low)
+        )
 
     @pl.loop(0, 4)
     def _(at):
@@ -271,8 +284,9 @@
         grid_feat[at] = nn(kron_a[0], feat_pair) + nn(kron_a[1], feat_pair)
         cot_pair = pair(cot32, at).astype(BF16)
         d_product[at] = nn(kron_bt[0], cot_pair) + nn(kron_bt[1], cot_pair)
-
-    for number in range(5, 10):
+        joint[at] = grid_feat[at] * d_product[at]
+
+    for number in range(8, 13):
         loads[number].wait()
     for weight, mix in ((w1, mix1), (w2, mix2), (w3, mix3), (w4, mix4)):
         size = weight.shape[1]
@@ -298,23 +312,25 @@
 
     @pl.loop(0, 4)
     def _(at):
-        grid_agg = times(kron_a, pair(agg, at))
-        gate = jax.nn.sigmoid(grid_agg)
-        active = grid_agg * gate
-        slope = gate * (1.0 + grid_agg * (1.0 - gate))
-        feat_at = grid_feat[at]
-        d_at = d_product[at]
-        product[at] = active * feat_at
-        d_feat[at] = d_at * active
-        unpair(d_agg, at, times(kron_at, d_at * feat_at * slope) * EDGE_NORM)
-
-    for order in ORDER:
+        agg_pair = pair(agg, at).astype(BF16)
+        total = None
+        for begin, size in STRIPES:
+            stripe = slice(begin, begin + size)
+            rough = nn(kron_a[0, stripe, :], agg_pair)
+            grid_agg[at, stripe, :] = rough
+            gate = 0.5 + 0.5 * jnp.tanh(0.5 * rough)
+            slope = gate * (1.0 + rough * (1.0 - gate))
+            term = nn(kron_at[0, :, stripe], (joint[at, stripe, :] * slope).astype(BF16))
+            total = term if total is None else total + term
+        unpair(d_agg, at, total * EDGE_NORM)
+
+    for order in BACK_ORDER:
         first, rows, lanes = SPANS[order]
         d_rows = d_agg[first // CH : (first + rows) // CH].reshape(rows, ATOMS).astype(BF16)
         d_message = nt(pick_target_t[...], d_rows).astype(BF16)
         d_filtered = nn(d_message, mixes[order][...])
         high, low = parts(d_filtered * harm_t[:, first : first + rows], 2)
-        ghosts = nn(pick_source[ATOMS:, :], high) + nn(pick_source[ATOMS:, :], low)
+        ghosts = nn(pick_source[ATOMS:, :], high)
         backs[order][:, :, 0:rows] = ghosts.astype(BF16).reshape(8, GHOST, rows)
         for index in SEND_DIRS:
             copy = pltpu.make_async_remote_copy(
@@ -333,12 +349,26 @@
 
     @pl.loop(0, 4)
     def _(at):
-        unpair(feat32, at, pair(feat32, at) + times(kron_b, product[at]))
-        unpair(cot32, at, pair(cot32, at) + times(kron_at, d_feat[at]))
+        agg_high, agg_low = parts(pair(agg, at), 2)
+        update = None
+        for begin, size in STRIPES:
+            stripe = slice(begin, begin + size)
+            exact = (
+                grid_agg[at, stripe, :]
+                + nn(kron_a[1, stripe, :], agg_high)
+                + nn(kron_a[0, stripe, :], agg_low)
+            )
+            active = exact * jax.nn.sigmoid(exact)
+            made = times(kron_b, active * grid_feat[at, stripe, :], stripe)
+            back = times(kron_at, active * d_product[at, stripe, :], stripe)
+            update = made if update is None else update + made
+            d_node = back if begin == 0 else d_node + back
+        unpair(feat32, at, pair(feat32, at) + update)
+        unpair(cot32, at, pair(cot32, at) + d_node)
 
     layer_ref[...] = feat32[...].reshape(ROWS, ATOMS).astype(BF16)
 
-    for order in ORDER:
+    for order in BACK_ORDER:
         first, rows, lanes = SPANS[order]
         for index in SEND_DIRS:
             returning[order, index].wait_recv()
@@ -368,8 +398,8 @@
 ):
     count_x = lax.axis_size("gx")
     count_y = lax.axis_size("gy")
-    in_hbm = pl.BlockSpec(memory_space=pl.ANY)
-    in_vmem = pl.BlockSpec(memory_space=pltpu.VMEM)
+    in_hbm = pl.BlockSpec(memory_space=pltpu.HBM)
+    vmem = pl.BlockSpec(memory_space=pltpu.VMEM)
     grids = pltpu.VMEM((4, GRID * 8, 2 * ATOMS), F32)
     tiles = pltpu.VMEM((COEFS, 8, 8, ATOMS), F32)
     tall = pltpu.VMEM((2, GRID * 8, COEFS * 8), BF16)
@@ -382,8 +412,8 @@
             jax.ShapeDtypeStruct((ROWS, ATOMS), BF16),
             jax.ShapeDtypeStruct((ROWS, ATOMS), F32),
         ),
-        in_specs=[in_hbm] * 10 + [in_vmem] * 3,
-        out_specs=(in_vmem, in_vmem),
+        in_specs=[in_hbm] * 13,
+        out_specs=(vmem, vmem),
         scratch_shapes=[
             pltpu.VMEM((ROWS, ATOMS), BF16),
             pltpu.VMEM((ROWS, ATOMS), BF16),
@@ -392,9 +422,12 @@
             pltpu.VMEM(w_order2.shape, BF16),
             pltpu.VMEM(w_order3.shape, BF16),
             pltpu.VMEM(w_order4.shape, BF16),
-            pltpu.VMEM((GRID, COEFS), F32),
+            pltpu.VMEM((COEFS, GRID), F32),
             pltpu.VMEM((COEFS, GRID), F32),
             pltpu.VMEM((COEFS, EDGES), F32),
+            pltpu.VMEM((1, EDGES), jnp.int32),
+            pltpu.VMEM((1, EDGES), jnp.int32),
+            pltpu.VMEM((8, GHOST), jnp.int32),
             tiles,
             tiles,
             *blocks,
@@ -419,30 +452,35 @@
             tiles,
             tiles,
             pltpu.VMEM((ATOMS, ROWS), F32),
-            pltpu.SemaphoreType.DMA((10,)),
+            pltpu.SemaphoreType.DMA((13,)),
             copies,
             copies,
             copies,
             copies,
         ],
         compiler_params=pltpu.CompilerParams(
-            collective_id=0, has_side_effects=True, vmem_limit_bytes=56 * 1024 * 1024
+            collective_id=0, has_side_effects=True, vmem_limit_bytes=40 * 1024 * 1024
         ),
         name="layer",
     )(
-        features[0, 0],
-        cotangent[0, 0],
-        w_order0,
-        w_order1,
-        w_order2,
-        w_order3,
-        w_order4,
-        to_grid,
-        from_grid,
-        edge_harmonics[0, 0],
-        edge_source[0],
-        edge_target[0],
-        send_list[0, 0],
+        *[
+            pltpu.with_memory_space_constraint(value, pltpu.HBM)
+            for value in (
+                features[0, 0],
+                cotangent[0, 0],
+                w_order0,
+                w_order1,
+                w_order2,
+                w_order3,
+                w_order4,
+                to_grid.T,
+                from_grid,
+                edge_harmonics[0, 0].reshape(COEFS, 1, EDGES),
+                edge_source[0],
+                edge_target[0],
+                send_list[0, 0],
+            )
+        ],
     )
     return layer[None, None], grad[None, None]
 

time: 54.4 us -> 45.6 us (0.84)
  Pallas kernels: 48.7 us -> 43.2 us
  local copies, waits for them, and re-layouts: 4.84 us -> 1.64 us
    pallas_call x1, Pallas kernels: 48.7 us -> 43.2 us  [per_device(): pl.pallas_call(functools.partial(kernel, count_x, count_y), out_shape=(ja...]
    unnamed x8 -> x2, local copies, waits for them, and re-layouts: 4.84 us -> 1.64 us
where the time goes in v1:
time: 45.6 us; the launch traced here: 45.4 us
  Pallas kernels  43.2 us (95%)
  local copies, waits for them, and re-layouts  1.64 us (4%)
  between operations  0.64 us (1%)
    pallas_call x1, Pallas kernels, per_device(): pl.pallas_call(functools.partial(kernel, count_x, count_y), out_shape=(ja...  43.2 us
    unnamed x2, local copies, waits for them, and re-layouts  1.64 us

profile of v1, /device:TPU:1, one launch (start us, length us, event | category | flops | bytes accessed | tf_op | source)
XLA Modules:
  0.0 45.4 jit_solution(5124529177855630149)
XLA Ops:
  0.6 43.2 %layer.1 = (bf16[1600,128]{1,0:T(8,128)(2,1)S(1)}, f32[1600,128]{1,0:T(8,128)S(1)}) custom-call(bf16[1600,128]{1,0:T(8,128)(2,1)} %bitcast.11, bf16[1600,128]{1,0:T(8,128)(2,1)} %bitcast.12, bf16[320,320]{1,0:T(8,128)(2,1)} %w0_hbm.1, bf16[2,256,256]{2,1,0:T(8,128)(2,1)} %w1_hbm.1, bf16[2,192,192]{2,1,0:T(8,128)(2,1)} %w2_hbm.1, ...), custom_call_target="tpu_custom_call" | custom-call | tf_op jit(solution)/shard_map/layer/pallas_call | solution.py:409
  43.8 0.8 %copy.17 = bf16[1,1,1600,128]{3,2,1,0:T(8,128)(2,1)} copy(bf16[1,1,1600,128]{3,2,1,0:T(8,128)(2,1)S(1)} %bitcast.10) | data formatting | bytes 819200
  44.5 0.9 %copy.18 = f32[1,1,1600,128]{3,2,1,0:T(8,128)} copy(f32[1,1,1600,128]{3,2,1,0:T(8,128)S(1)} %bitcast.9) | data formatting | bytes 1638400

commit v2 on v1

--- a/solution.py
+++ b/solution.py
@@ -21,11 +21,15 @@
 GHOST = 32
 ROWS = COEFS * CH
 GHOSTS = 8 * GHOST
-SPANS = ((0, 320, 384), (320, 512, 512), (832, 384, 384), (1216, 256, 256), (1472, 128, 128))
+SPANS = ((0, 320, 256), (320, 512, 512), (832, 384, 384), (1216, 256, 256), (1472, 128, 128))
 ORDER = (3, 0, 1, 2, 4)
 BACK_ORDER = (4, 0, 1, 2, 3)
 STRIPES = ((0, 256), (256, 256), (512, 256), (768, 32))
 SEND_DIRS = (0, 2, 5, 7, 1, 6, 3, 4)
+LEND_FIRST = (0, 2, 1)
+LEND_REST = (5, 7, 6, 3, 4)
+RETURN_FIRST = (5, 7, 6)
+RETURN_REST = (0, 2, 1, 3, 4)
 
 
 def nn(left, right):
@@ -96,21 +100,25 @@
     out2,
     out3,
     out4,
+    out5,
     in0,
     in1,
     in2,
     in3,
     in4,
+    in5,
     back0,
     back1,
     back2,
     back3,
     back4,
+    back5,
     home0,
     home1,
     home2,
     home3,
     home4,
+    home5,
     mix1,
     mix2,
     mix3,
@@ -133,15 +141,16 @@
     d_agg,
     own_t,
     local_sem,
+    feat_sem,
     out_sem,
     in_sem,
     back_sem,
     home_sem,
 ):
-    outs = (out0, out1, out2, out3, out4)
-    ins = (in0, in1, in2, in3, in4)
-    backs = (back0, back1, back2, back3, back4)
-    homes = (home0, home1, home2, home3, home4)
+    outs = (out0, out1, out2, out3, out4, out5)
+    ins = (in0, in1, in2, in3, in4, in5)
+    backs = (back0, back1, back2, back3, back4, back5)
+    homes = (home0, home1, home2, home3, home4, home5)
     mixes = (w0, mix1, mix2, mix3, mix4)
 
     at_x = lax.axis_index("gx")
@@ -154,12 +163,43 @@
             lax.rem(at_y + (sign * step_y + count_y), count_y),
         )
 
+    def pieces(order):
+        return (0, 5) if order == 0 else (order,)
+
+    def stage(buffers, order, value):
+        lanes = SPANS[order][2]
+        value = value.reshape(8, GHOST, SPANS[order][1])
+        buffers[order][...] = value[:, :, 0:lanes].astype(BF16)
+        if order == 0:
+            left = value[:, :, lanes:]
+            half = GHOST // 2
+            buffers[5][...] = jnp.concatenate(
+                [left[:, 0:half], left[:, half:]], axis=2
+            ).astype(BF16)
+
+    def staged(buffers, order):
+        lanes = SPANS[order][2]
+        value = buffers[order][...].reshape(GHOSTS, lanes)
+        if order == 0:
+            packed = buffers[5][...].astype(F32)
+            left = jnp.concatenate([packed[:, :, 0:CH], packed[:, :, CH:]], axis=1)
+            left = left.reshape(GHOSTS, CH).astype(BF16)
+            value = jnp.concatenate([value, left], axis=1)
+        return value
+
+    feat_loads = {
+        order: pltpu.make_async_copy(
+            feat_hbm.at[SPANS[order][0] : SPANS[order][0] + SPANS[order][1]],
+            feat.at[SPANS[order][0] : SPANS[order][0] + SPANS[order][1]],
+            feat_sem.at[order],
+        )
+        for order in ORDER
+    }
     loads = [
         pltpu.make_async_copy(source, target, local_sem.at[number])
         for number, (source, target) in enumerate(
             (
                 (list_hbm, list_ref),
-                (feat_hbm, feat),
                 (source_hbm, source_ref),
                 (target_hbm, target_ref),
                 (harm_hbm.at[:, 0], harm),
@@ -174,7 +214,7 @@
             )
         )
     ]
-    for load in loads:
+    for load in (loads[0], *feat_loads.values(), *loads[1:]):
         load.start()
 
     barrier = pltpu.get_barrier_semaphore()
@@ -192,32 +232,53 @@
     eye = identity(256)
     pick_list_t = nt(eye, pick_list[...]).astype(BF16)
 
-    loads[1].wait()
-
     lending = {}
     returning = {}
+    waiting = None
     started = False
+
+    def lend(order, directions):
+        for index in directions:
+            for piece in pieces(order):
+                copy = pltpu.make_async_remote_copy(
+                    src_ref=outs[piece].at[index],
+                    dst_ref=ins[piece].at[index],
+                    send_sem=out_sem.at[piece, index],
+                    recv_sem=in_sem.at[piece, index],
+                    device_id=cell(index, -1),
+                    device_id_type=MESH,
+                )
+                copy.start()
+                lending[piece, index] = copy
+
+    def give_back(order, directions):
+        for index in directions:
+            for piece in pieces(order):
+                copy = pltpu.make_async_remote_copy(
+                    src_ref=backs[piece].at[index],
+                    dst_ref=homes[piece].at[index],
+                    send_sem=back_sem.at[piece, index],
+                    recv_sem=home_sem.at[piece, index],
+                    device_id=cell(index, 1),
+                    device_id_type=MESH,
+                )
+                copy.start()
+                returning[piece, index] = copy
+
     for order in ORDER:
         first, rows, lanes = SPANS[order]
-        lent = nt(pick_list_t, feat[first : first + rows, :]).astype(BF16)
-        outs[order][:, :, 0:rows] = lent.reshape(8, GHOST, rows)
+        feat_loads[order].wait()
+        stage(outs, order, nt(pick_list_t, feat[first : first + rows, :]))
         if not started:
             pl.semaphore_wait(barrier, 8)
             started = True
-        for index in SEND_DIRS:
-            copy = pltpu.make_async_remote_copy(
-                src_ref=outs[order].at[index],
-                dst_ref=ins[order].at[index],
-                send_sem=out_sem.at[order, index],
-                recv_sem=in_sem.at[order, index],
-                device_id=cell(index, -1),
-                device_id_type=MESH,
-            )
-            copy.start()
-            lending[order, index] = copy
-
+        lend(order, LEND_FIRST)
+
+    for order in ORDER:
+        lend(order, LEND_REST)
+
+    loads[1].wait()
     loads[2].wait()
-    loads[3].wait()
     pick_source[...] = ones_where(
         iota((ATOMS + GHOSTS, EDGES), 0) == source_ref[...]
     ).astype(BF16)
@@ -225,7 +286,7 @@
     pick_source_t[...] = nt(eye, pick_source[...]).astype(BF16)
     pick_target_t[...] = nt(eye, pick_target[...]).astype(BF16)
 
-    loads[4].wait()
+    loads[3].wait()
     harm_parts = [nt(eye, piece).astype(BF16) for piece in parts(harm[...], 3)]
     for order in ORDER:
         first, rows, lanes = SPANS[order]
@@ -235,8 +296,8 @@
         wide = nn(harm_parts[0], spread) + nn(harm_parts[1], spread) + nn(harm_parts[2], spread)
         harm_t[:, first : first + rows] = wide
 
+    loads[4].wait()
     loads[5].wait()
-    loads[6].wait()
     grid_rows = ones_where((iota((GRID * 8, GRID), 0) >> 3) == iota((GRID * 8, GRID), 1)).astype(BF16)
     grid_cols = ones_where((iota((GRID, GRID * 8), 1) >> 3) == iota((GRID, GRID * 8), 0)).astype(BF16)
     coef_rows = ones_where((iota((COEFS * 8, COEFS), 0) >> 3) == iota((COEFS * 8, COEFS), 1)).astype(BF16)
@@ -258,7 +319,7 @@
         ).astype(BF16)
 
     feat32[...] = feat[...].astype(F32).reshape(COEFS, 8, 8, ATOMS)
-    loads[7].wait()
+    loads[6].wait()
     cot32[...] = cot[...].astype(F32).reshape(COEFS, 8, 8, ATOMS)
 
     def pair(ref, at):
@@ -284,9 +345,9 @@
         grid_feat[at] = nn(kron_a[0], feat_pair) + nn(kron_a[1], feat_pair)
         cot_pair = pair(cot32, at).astype(BF16)
         d_product[at] = nn(kron_bt[0], cot_pair) + nn(kron_bt[1], cot_pair)
-        joint[at] = grid_feat[at] * d_product[at]
-
-    for number in range(8, 13):
+        joint[at] = (0.5 * EDGE_NORM) * grid_feat[at] * d_product[at]
+
+    for number in range(7, 12):
         loads[number].wait()
     for weight, mix in ((w1, mix1), (w2, mix2), (w3, mix3), (w4, mix4)):
         size = weight.shape[1]
@@ -299,14 +360,14 @@
         first, rows, lanes = SPANS[order]
         columns = nt(pick_source_t[:, 0:ATOMS], feat[first : first + rows, :])
         for index in SEND_DIRS:
-            lending[order, index].wait_recv()
-        ghosts = ins[order][...].reshape(GHOSTS, lanes)[:, 0:rows]
-        columns = columns + nn(pick_source_t[:, ATOMS:], ghosts)
+            for piece in pieces(order):
+                lending[piece, index].wait_recv()
+        columns = columns + nn(pick_source_t[:, ATOMS:], staged(ins, order))
         filtered = (columns * harm_t[:, first : first + rows]).astype(BF16)
         message = nt(mixes[order][...], filtered)
         high, low = parts(message, 2)
         total = nt(high, pick_target[...]) + nt(low, pick_target[...])
-        agg[first // CH : (first + rows) // CH] = (total * EDGE_NORM).reshape(
+        agg[first // CH : (first + rows) // CH] = (total * (0.5 * EDGE_NORM)).reshape(
             rows // CH, 8, 8, ATOMS
         )
 
@@ -318,11 +379,11 @@
             stripe = slice(begin, begin + size)
             rough = nn(kron_a[0, stripe, :], agg_pair)
             grid_agg[at, stripe, :] = rough
-            gate = 0.5 + 0.5 * jnp.tanh(0.5 * rough)
-            slope = gate * (1.0 + rough * (1.0 - gate))
+            turn = jnp.tanh(rough)
+            slope = (1.0 + turn) * (1.0 + rough * (1.0 - turn))
             term = nn(kron_at[0, :, stripe], (joint[at, stripe, :] * slope).astype(BF16))
             total = term if total is None else total + term
-        unpair(d_agg, at, total * EDGE_NORM)
+        unpair(d_agg, at, total)
 
     for order in BACK_ORDER:
         first, rows, lanes = SPANS[order]
@@ -331,21 +392,19 @@
         d_filtered = nn(d_message, mixes[order][...])
         high, low = parts(d_filtered * harm_t[:, first : first + rows], 2)
         ghosts = nn(pick_source[ATOMS:, :], high)
-        backs[order][:, :, 0:rows] = ghosts.astype(BF16).reshape(8, GHOST, rows)
-        for index in SEND_DIRS:
-            copy = pltpu.make_async_remote_copy(
-                src_ref=backs[order].at[index],
-                dst_ref=homes[order].at[index],
-                send_sem=back_sem.at[order, index],
-                recv_sem=home_sem.at[order, index],
-                device_id=cell(index, 1),
-                device_id_type=MESH,
-            )
-            copy.start()
-            returning[order, index] = copy
+        stage(backs, order, ghosts)
+        give_back(order, RETURN_FIRST)
+        if waiting is not None:
+            give_back(waiting, RETURN_REST)
+        waiting = order
+        if order == BACK_ORDER[0]:
+            give_back(waiting, RETURN_REST)
+            waiting = None
         own_t[:, first : first + rows] = nn(pick_source[0:ATOMS, :], high) + nn(
             pick_source[0:ATOMS, :], low
         )
+
+    give_back(waiting, RETURN_REST)
 
     @pl.loop(0, 4)
     def _(at):
@@ -358,6 +417,7 @@
                 + nn(kron_a[1, stripe, :], agg_high)
                 + nn(kron_a[0, stripe, :], agg_low)
             )
+            exact = exact + exact
             active = exact * jax.nn.sigmoid(exact)
             made = times(kron_b, active * grid_feat[at, stripe, :], stripe)
             back = times(kron_at, active * d_product[at, stripe, :], stripe)
@@ -371,14 +431,26 @@
     for order in BACK_ORDER:
         first, rows, lanes = SPANS[order]
         for index in SEND_DIRS:
-            returning[order, index].wait_recv()
-        arrived = homes[order][...].reshape(GHOSTS, lanes)[:, 0:rows]
+            for piece in pieces(order):
+                returning[piece, index].wait_recv()
+        arrived = staged(homes, order)
         total = own_t[:, first : first + rows] + nn(pick_list[...], arrived)
         node = cot32[first // CH : (first + rows) // CH].reshape(rows, ATOMS)
         grad_ref[first : first + rows, :] = node + jnp.transpose(total)
 
     for copy in (*lending.values(), *returning.values()):
         copy.wait_send()
+
+
+def store_kernel(layer_ref, grad_ref, layer_hbm, grad_hbm, sem):
+    copies = [
+        pltpu.make_async_copy(layer_ref, layer_hbm, sem.at[0]),
+        pltpu.make_async_copy(grad_ref, grad_hbm, sem.at[1]),
+    ]
+    for copy in copies:
+        copy.start()
+    for copy in copies:
+        copy.wait()
 
 
 def per_device(
@@ -405,7 +477,8 @@
     tall = pltpu.VMEM((2, GRID * 8, COEFS * 8), BF16)
     flat = pltpu.VMEM((2, COEFS * 8, GRID * 8), BF16)
     blocks = [pltpu.VMEM((8, GHOST, lanes), BF16) for _, _, lanes in SPANS]
-    copies = pltpu.SemaphoreType.DMA((5, 8))
+    blocks.append(pltpu.VMEM((8, GHOST // 2, ATOMS), BF16))
+    copies = pltpu.SemaphoreType.DMA((6, 8))
     layer, grad = pl.pallas_call(
         functools.partial(kernel, count_x, count_y),
         out_shape=(
@@ -452,7 +525,8 @@
             tiles,
             tiles,
             pltpu.VMEM((ATOMS, ROWS), F32),
-            pltpu.SemaphoreType.DMA((13,)),
+            pltpu.SemaphoreType.DMA((12,)),
+            pltpu.SemaphoreType.DMA((5,)),
             copies,
             copies,
             copies,
@@ -482,6 +556,18 @@
             )
         ],
     )
+    layer, grad = pl.pallas_call(
+        store_kernel,
+        out_shape=(
+            jax.ShapeDtypeStruct((ROWS, ATOMS), BF16),
+            jax.ShapeDtypeStruct((ROWS, ATOMS), F32),
+        ),
+        in_specs=[vmem, vmem],
+        out_specs=(in_hbm, in_hbm),
+        scratch_shapes=[pltpu.SemaphoreType.DMA((2,))],
+        compiler_params=pltpu.CompilerParams(vmem_limit_bytes=4 * 1024 * 1024),
+        name="store",
+    )(layer, grad)
     return layer[None, None], grad[None, None]
 
 

time: 45.6 us -> 45.8 us (level)
  local copies, waits for them, and re-layouts: 1.64 us -> 0 us
  Pallas kernels: 43.2 us -> 44.8 us
    unnamed x2 -> x0, local copies, waits for them, and re-layouts: 1.64 us -> none
    pallas_call x0 -> x1, Pallas kernels: none -> 1.05 us  [per_device(): pl.pallas_call(store_kernel, out_shape=(jax.ShapeDtypeStruct((ROWS, ATOMS...]
    pallas_call x1, Pallas kernels: 43.2 us -> 43.8 us  [per_device(): pl.pallas_call(functools.partial(kernel, count_x, count_y), out_shape=(ja...]
where the time goes in v2:
time: 45.8 us; the launch traced here: 45.6 us
  Pallas kernels  44.8 us (98%)
  between operations  0.8 us (2%)
    pallas_call x1, Pallas kernels, per_device(): pl.pallas_call(functools.partial(kernel, count_x, count_y), out_shape=(ja...  43.8 us
    pallas_call x1, Pallas kernels, per_device(): pl.pallas_call(store_kernel, out_shape=(jax.ShapeDtypeStruct((ROWS, ATOMS...  1.05 us

profile of v2, /device:TPU:1, one launch (start us, length us, event | category | flops | bytes accessed | tf_op | source)
XLA Modules:
  0.0 45.6 jit_solution(11309014255480442990)
XLA Ops:
  0.6 43.8 %layer.1 = (bf16[1600,128]{1,0:T(8,128)(2,1)S(1)}, f32[1600,128]{1,0:T(8,128)S(1)}) custom-call(bf16[1600,128]{1,0:T(8,128)(2,1)} %bitcast.9, bf16[1600,128]{1,0:T(8,128)(2,1)} %bitcast.10, bf16[320,320]{1,0:T(8,128)(2,1)} %w0_hbm.1, bf16[2,256,256]{2,1,0:T(8,128)(2,1)} %w1_hbm.1, bf16[2,192,192]{2,1,0:T(8,128)(2,1)} %w2_hbm.1, bf16[2,128,128]{2,1,0:T(8,128)(2,1)} %w3_hbm.1, ...), custom_call_target="tpu_custom_call" | custom-call | tf_op jit(solution)/shard_map/layer/pallas_call | solution.py:482
  44.4 1.0 %store.1 = (bf16[1600,128]{1,0:T(8,128)(2,1)}, f32[1600,128]{1,0:T(8,128)}) custom-call(bf16[1600,128]{1,0:T(8,128)(2,1)S(1)} %get-tuple-element.6.layer_ref, f32[1600,128]{1,0:T(8,128)S(1)} %get-tuple-element.7.grad_ref), custom_call_target="tpu_custom_call" | custom-call | tf_op jit(solution)/shard_map/store/pallas_call | solution.py:559

commit v3 on v2

--- a/solution.py
+++ b/solution.py
@@ -21,15 +21,13 @@
 GHOST = 32
 ROWS = COEFS * CH
 GHOSTS = 8 * GHOST
-SPANS = ((0, 320, 256), (320, 512, 512), (832, 384, 384), (1216, 256, 256), (1472, 128, 128))
-ORDER = (3, 0, 1, 2, 4)
-BACK_ORDER = (4, 0, 1, 2, 3)
+SPANS = ((0, 320), (320, 512), (832, 384), (1216, 256), (1472, 128))
+PLACES = ((0, 80), (80, 128), (272, 96), (208, 64), (368, 32))
+WIRE = 400
+LEND_PIECES = ((0, 1, 3), (2,), (4,))
+BACK_PIECES = ((4,), (0,), (1,), (2,), (3,))
 STRIPES = ((0, 256), (256, 256), (512, 256), (768, 32))
 SEND_DIRS = (0, 2, 5, 7, 1, 6, 3, 4)
-LEND_FIRST = (0, 2, 1)
-LEND_REST = (5, 7, 6, 3, 4)
-RETURN_FIRST = (5, 7, 6)
-RETURN_REST = (0, 2, 1, 3, 4)
 
 
 def nn(left, right):
@@ -95,30 +93,10 @@
     list_ref,
     feat32,
     cot32,
-    out0,
-    out1,
-    out2,
-    out3,
-    out4,
-    out5,
-    in0,
-    in1,
-    in2,
-    in3,
-    in4,
-    in5,
-    back0,
-    back1,
-    back2,
-    back3,
-    back4,
-    back5,
-    home0,
-    home1,
-    home2,
-    home3,
-    home4,
-    home5,
+    outs,
+    ins,
+    backs,
+    homes,
     mix1,
     mix2,
     mix3,
@@ -147,10 +125,6 @@
     back_sem,
     home_sem,
 ):
-    outs = (out0, out1, out2, out3, out4, out5)
-    ins = (in0, in1, in2, in3, in4, in5)
-    backs = (back0, back1, back2, back3, back4, back5)
-    homes = (home0, home1, home2, home3, home4, home5)
     mixes = (w0, mix1, mix2, mix3, mix4)
 
     at_x = lax.axis_index("gx")
@@ -163,29 +137,50 @@
             lax.rem(at_y + (sign * step_y + count_y), count_y),
         )
 
-    def pieces(order):
-        return (0, 5) if order == 0 else (order,)
-
-    def stage(buffers, order, value):
-        lanes = SPANS[order][2]
-        value = value.reshape(8, GHOST, SPANS[order][1])
-        buffers[order][...] = value[:, :, 0:lanes].astype(BF16)
-        if order == 0:
-            left = value[:, :, lanes:]
+    def stage(buffer, order, value):
+        begin, _ = PLACES[order]
+        rows = SPANS[order][1]
+        value = value.reshape(8, GHOST, rows)
+        for at in range(0, rows - ATOMS + 1, ATOMS):
+            buffer[:, begin : begin + GHOST, :] = value[:, :, at : at + ATOMS].astype(BF16)
+            begin += GHOST
+        if rows % ATOMS:
+            left = value[:, :, rows - CH :]
             half = GHOST // 2
-            buffers[5][...] = jnp.concatenate(
+            buffer[:, begin : begin + half, :] = jnp.concatenate(
                 [left[:, 0:half], left[:, half:]], axis=2
             ).astype(BF16)
 
-    def staged(buffers, order):
-        lanes = SPANS[order][2]
-        value = buffers[order][...].reshape(GHOSTS, lanes)
-        if order == 0:
-            packed = buffers[5][...].astype(F32)
+    def staged(buffer, order):
+        begin, _ = PLACES[order]
+        rows = SPANS[order][1]
+        tiles = []
+        for _ in range(rows // ATOMS):
+            tiles.append(buffer[:, begin : begin + GHOST, :].reshape(GHOSTS, ATOMS))
+            begin += GHOST
+        if rows % ATOMS:
+            packed = buffer[:, begin : begin + GHOST // 2, :].astype(F32)
             left = jnp.concatenate([packed[:, :, 0:CH], packed[:, :, CH:]], axis=1)
-            left = left.reshape(GHOSTS, CH).astype(BF16)
-            value = jnp.concatenate([value, left], axis=1)
-        return value
+            tiles.append(left.reshape(GHOSTS, CH).astype(BF16))
+        return jnp.concatenate(tiles, axis=1) if len(tiles) > 1 else tiles[0]
+
+    def exchange(piece, number, source, target, send_sem, recv_sem, sign):
+        begin = PLACES[piece[0]][0]
+        end = sum(PLACES[piece[-1]])
+        copies = [
+            pltpu.make_async_remote_copy(
+                src_ref=source.at[index, begin:end],
+                dst_ref=target.at[index, begin:end],
+                send_sem=send_sem.at[number, index],
+                recv_sem=recv_sem.at[number, index],
+                device_id=cell(index, sign),
+                device_id_type=MESH,
+            )
+            for index in SEND_DIRS
+        ]
+        for copy in copies:
+            copy.start()
+        return copies
 
     feat_loads = {
         order: pltpu.make_async_copy(
@@ -193,7 +188,7 @@
             feat.at[SPANS[order][0] : SPANS[order][0] + SPANS[order][1]],
             feat_sem.at[order],
         )
-        for order in ORDER
+        for order in range(5)
     }
     loads = [
         pltpu.make_async_copy(source, target, local_sem.at[number])
@@ -232,50 +227,15 @@
     eye = identity(256)
     pick_list_t = nt(eye, pick_list[...]).astype(BF16)
 
-    lending = {}
-    returning = {}
-    waiting = None
-    started = False
-
-    def lend(order, directions):
-        for index in directions:
-            for piece in pieces(order):
-                copy = pltpu.make_async_remote_copy(
-                    src_ref=outs[piece].at[index],
-                    dst_ref=ins[piece].at[index],
-                    send_sem=out_sem.at[piece, index],
-                    recv_sem=in_sem.at[piece, index],
-                    device_id=cell(index, -1),
-                    device_id_type=MESH,
-                )
-                copy.start()
-                lending[piece, index] = copy
-
-    def give_back(order, directions):
-        for index in directions:
-            for piece in pieces(order):
-                copy = pltpu.make_async_remote_copy(
-                    src_ref=backs[piece].at[index],
-                    dst_ref=homes[piece].at[index],
-                    send_sem=back_sem.at[piece, index],
-                    recv_sem=home_sem.at[piece, index],
-                    device_id=cell(index, 1),
-                    device_id_type=MESH,
-                )
-                copy.start()
-                returning[piece, index] = copy
-
-    for order in ORDER:
-        first, rows, lanes = SPANS[order]
-        feat_loads[order].wait()
-        stage(outs, order, nt(pick_list_t, feat[first : first + rows, :]))
-        if not started:
+    lending = []
+    for number, piece in enumerate(LEND_PIECES):
+        for order in piece:
+            first, rows = SPANS[order]
+            feat_loads[order].wait()
+            stage(outs, order, nt(pick_list_t, feat[first : first + rows, :]))
+        if number == 0:
             pl.semaphore_wait(barrier, 8)
-            started = True
-        lend(order, LEND_FIRST)
-
-    for order in ORDER:
-        lend(order, LEND_REST)
+        lending.append(exchange(piece, number, outs, ins, out_sem, in_sem, -1))
 
     loads[1].wait()
     loads[2].wait()
@@ -288,8 +248,8 @@
 
     loads[3].wait()
     harm_parts = [nt(eye, piece).astype(BF16) for piece in parts(harm[...], 3)]
-    for order in ORDER:
-        first, rows, lanes = SPANS[order]
+    for order in range(5):
+        first, rows = SPANS[order]
         spread = ones_where(
             ((iota((COEFS, rows), 1) + first) >> 6) == iota((COEFS, rows), 0)
         ).astype(BF16)
@@ -356,20 +316,23 @@
         mix[0:size, :] = (nn(weight[0], left) - nn(weight[1], right)).astype(BF16)
         mix[size : 2 * size, :] = (nn(weight[1], left) + nn(weight[0], right)).astype(BF16)
 
-    for order in ORDER:
-        first, rows, lanes = SPANS[order]
-        columns = nt(pick_source_t[:, 0:ATOMS], feat[first : first + rows, :])
-        for index in SEND_DIRS:
-            for piece in pieces(order):
-                lending[piece, index].wait_recv()
-        columns = columns + nn(pick_source_t[:, ATOMS:], staged(ins, order))
-        filtered = (columns * harm_t[:, first : first + rows]).astype(BF16)
-        message = nt(mixes[order][...], filtered)
-        high, low = parts(message, 2)
-        total = nt(high, pick_target[...]) + nt(low, pick_target[...])
-        agg[first // CH : (first + rows) // CH] = (total * (0.5 * EDGE_NORM)).reshape(
-            rows // CH, 8, 8, ATOMS
-        )
+    for piece, copies in zip(LEND_PIECES, lending):
+        ready = False
+        for order in piece:
+            first, rows = SPANS[order]
+            columns = nt(pick_source_t[:, 0:ATOMS], feat[first : first + rows, :])
+            if not ready:
+                for copy in copies:
+                    copy.wait_recv()
+                ready = True
+            columns = columns + nn(pick_source_t[:, ATOMS:], staged(ins, order))
+            filtered = (columns * harm_t[:, first : first + rows]).astype(BF16)
+            message = nt(mixes[order][...], filtered)
+            high, low = parts(message, 2)
+            total = nt(high, pick_target[...]) + nt(low, pick_target[...])
+            agg[first // CH : (first + rows) // CH] = (total * (0.5 * EDGE_NORM)).reshape(
+                rows // CH, 8, 8, ATOMS
+            )
 
     @pl.loop(0, 4)
     def _(at):
@@ -385,26 +348,20 @@
             total = term if total is None else total + term
         unpair(d_agg, at, total)
 
-    for order in BACK_ORDER:
-        first, rows, lanes = SPANS[order]
+    returning = []
+    for number, piece in enumerate(BACK_PIECES):
+        order = piece[0]
+        first, rows = SPANS[order]
         d_rows = d_agg[first // CH : (first + rows) // CH].reshape(rows, ATOMS).astype(BF16)
         d_message = nt(pick_target_t[...], d_rows).astype(BF16)
         d_filtered = nn(d_message, mixes[order][...])
         high, low = parts(d_filtered * harm_t[:, first : first + rows], 2)
         ghosts = nn(pick_source[ATOMS:, :], high)
         stage(backs, order, ghosts)
-        give_back(order, RETURN_FIRST)
-        if waiting is not None:
-            give_back(waiting, RETURN_REST)
-        waiting = order
-        if order == BACK_ORDER[0]:
-            give_back(waiting, RETURN_REST)
-            waiting = None
+        returning.append(exchange(piece, number, backs, homes, back_sem, home_sem, 1))
         own_t[:, first : first + rows] = nn(pick_source[0:ATOMS, :], high) + nn(
             pick_source[0:ATOMS, :], low
         )
-
-    give_back(waiting, RETURN_REST)
 
     @pl.loop(0, 4)
     def _(at):
@@ -428,18 +385,18 @@
 
     layer_ref[...] = feat32[...].reshape(ROWS, ATOMS).astype(BF16)
 
-    for order in BACK_ORDER:
-        first, rows, lanes = SPANS[order]
-        for index in SEND_DIRS:
-            for piece in pieces(order):
-                returning[piece, index].wait_recv()
+    for (order,), copies in zip(BACK_PIECES, returning):
+        first, rows = SPANS[order]
+        for copy in copies:
+            copy.wait_recv()
         arrived = staged(homes, order)
         total = own_t[:, first : first + rows] + nn(pick_list[...], arrived)
         node = cot32[first // CH : (first + rows) // CH].reshape(rows, ATOMS)
         grad_ref[first : first + rows, :] = node + jnp.transpose(total)
 
-    for copy in (*lending.values(), *returning.values()):
-        copy.wait_send()
+    for copies in (*lending, *returning):
+        for copy in copies:
+            copy.wait_send()
 
 
 def store_kernel(layer_ref, grad_ref, layer_hbm, grad_hbm, sem):
@@ -476,9 +433,9 @@
     tiles = pltpu.VMEM((COEFS, 8, 8, ATOMS), F32)
     tall = pltpu.VMEM((2, GRID * 8, COEFS * 8), BF16)
     flat = pltpu.VMEM((2, COEFS * 8, GRID * 8), BF16)
-    blocks = [pltpu.VMEM((8, GHOST, lanes), BF16) for _, _, lanes in SPANS]
-    blocks.append(pltpu.VMEM((8, GHOST // 2, ATOMS), BF16))
-    copies = pltpu.SemaphoreType.DMA((6, 8))
+    blocks = pltpu.VMEM((8, WIRE, ATOMS), BF16)
+    lend_sems = pltpu.SemaphoreType.DMA((len(LEND_PIECES), 8))
+    back_sems = pltpu.SemaphoreType.DMA((len(BACK_PIECES), 8))
     layer, grad = pl.pallas_call(
         functools.partial(kernel, count_x, count_y),
         out_shape=(
@@ -503,11 +460,11 @@
             pltpu.VMEM((8, GHOST), jnp.int32),
             tiles,
             tiles,
-            *blocks,
-            *blocks,
-            *blocks,
-            *blocks,
-            *[pltpu.VMEM((rows, rows), BF16) for _, rows, _ in SPANS[1:]],
+            blocks,
+            blocks,
+            blocks,
+            blocks,
+            *[pltpu.VMEM((rows, rows), BF16) for _, rows in SPANS[1:]],
             pltpu.VMEM((EDGES, ROWS), F32),
             pltpu.VMEM((ATOMS, GHOSTS), BF16),
             pltpu.VMEM((ATOMS + GHOSTS, EDGES), BF16),
@@ -527,10 +484,10 @@
             pltpu.VMEM((ATOMS, ROWS), F32),
             pltpu.SemaphoreType.DMA((12,)),
             pltpu.SemaphoreType.DMA((5,)),
-            copies,
-            copies,
-            copies,
-            copies,
+            lend_sems,
+            lend_sems,
+            back_sems,
+            back_sems,
         ],
         compiler_params=pltpu.CompilerParams(
             collective_id=0, has_side_effects=True, vmem_limit_bytes=40 * 1024 * 1024

time: 45.8 us -> 44.4 us (0.969)
  Pallas kernels: 44.8 us -> 43.5 us
    pallas_call x1, Pallas kernels: 43.8 us -> 42.4 us  [per_device(): pl.pallas_call(functools.partial(kernel, count_x, count_y), out_shape=(ja...]
where the time goes in v3:
time: 44.4 us; the launch traced here: 44.3 us
  Pallas kernels  43.5 us (98%)
  between operations  0.8 us (2%)
    pallas_call x1, Pallas kernels, per_device(): pl.pallas_call(functools.partial(kernel, count_x, count_y), out_shape=(ja...  42.4 us
    pallas_call x1, Pallas kernels, per_device(): pl.pallas_call(store_kernel, out_shape=(jax.ShapeDtypeStruct((ROWS, ATOMS...  1.05 us

profile of v3, /device:TPU:1, one launch (start us, length us, event | category | flops | bytes accessed | tf_op | source)
XLA Modules:
  0.0 44.3 jit_solution(8400423974219406571)
XLA Ops:
  0.6 42.4 %layer.1 = (bf16[1600,128]{1,0:T(8,128)(2,1)S(1)}, f32[1600,128]{1,0:T(8,128)S(1)}) custom-call(bf16[1600,128]{1,0:T(8,128)(2,1)} %bitcast.9, bf16[1600,128]{1,0:T(8,128)(2,1)} %bitcast.10, bf16[320,320]{1,0:T(8,128)(2,1)} %w0_hbm.1, bf16[2,256,256]{2,1,0:T(8,128)(2,1)} %w1_hbm.1, bf16[2,192,192]{2,1,0:T(8,128)(2,1)} %w2_hbm.1, bf16[2,128,128]{2,1,0:T(8,128)(2,1)} %w3_hbm.1, ...), custom_call_target="tpu_custom_call" | custom-call | tf_op jit(solution)/shard_map/layer/pallas_call | solution.py:439
  43.1 1.0 %store.1 = (bf16[1600,128]{1,0:T(8,128)(2,1)}, f32[1600,128]{1,0:T(8,128)}) custom-call(bf16[1600,128]{1,0:T(8,128)(2,1)S(1)} %get-tuple-element.6.layer_ref, f32[1600,128]{1,0:T(8,128)S(1)} %get-tuple-element.7.grad_ref), custom_call_target="tpu_custom_call" | custom-call | tf_op jit(solution)/shard_map/store/pallas_call | solution.py:516

commit v4 on v3

--- a/solution.py
+++ b/solution.py
@@ -216,15 +216,13 @@
     for index in range(8):
         pl.semaphore_signal(barrier, inc=1, device_id=cell(index, 1), device_id_type=MESH)
 
+    eye = identity(256)
+    slots = ones_where(iota((GHOST, GHOSTS), 0) == (iota((GHOST, GHOSTS), 1) & 31)).astype(BF16)
+    slot_rows = iota((8, GHOSTS), 0) == (iota((8, GHOSTS), 1) >> 5)
     loads[0].wait()
-    list_row = nn(
-        list_ref[...].astype(F32).astype(BF16),
-        ones_where(iota((GHOST, GHOSTS), 0) == (iota((GHOST, GHOSTS), 1) & 31)).astype(BF16),
-    )
-    list_row = jnp.where(iota((8, GHOSTS), 0) == (iota((8, GHOSTS), 1) >> 5), list_row, 0.0)
-    list_row = jnp.sum(list_row, axis=0, keepdims=True)
+    list_row = nn(list_ref[...].astype(F32).astype(BF16), slots)
+    list_row = jnp.sum(jnp.where(slot_rows, list_row, 0.0), axis=0, keepdims=True)
     pick_list[...] = ones_where(iota((ATOMS, GHOSTS), 0).astype(F32) == list_row).astype(BF16)
-    eye = identity(256)
     pick_list_t = nt(eye, pick_list[...]).astype(BF16)
 
     lending = []
@@ -334,19 +332,24 @@
                 rows // CH, 8, 8, ATOMS
             )
 
-    @pl.loop(0, 4)
-    def _(at):
-        agg_pair = pair(agg, at).astype(BF16)
-        total = None
-        for begin, size in STRIPES:
-            stripe = slice(begin, begin + size)
-            rough = nn(kron_a[0, stripe, :], agg_pair)
-            grid_agg[at, stripe, :] = rough
-            turn = jnp.tanh(rough)
-            slope = (1.0 + turn) * (1.0 + rough * (1.0 - turn))
-            term = nn(kron_at[0, :, stripe], (joint[at, stripe, :] * slope).astype(BF16))
-            total = term if total is None else total + term
-        unpair(d_agg, at, total)
+    ahead = [(at, begin, size) for at in range(4) for begin, size in STRIPES]
+
+    def first_product(at, begin, size):
+        return nn(kron_a[0, begin : begin + size, :], pair(agg, at).astype(BF16))
+
+    rough_next = first_product(*ahead[0])
+    for step, (at, begin, size) in enumerate(ahead):
+        rough = rough_next
+        if step + 1 < len(ahead):
+            rough_next = first_product(*ahead[step + 1])
+        stripe = slice(begin, begin + size)
+        grid_agg[at, stripe, :] = rough
+        turn = jnp.tanh(rough)
+        slope = (1.0 + turn) * (1.0 + rough * (1.0 - turn))
+        term = nn(kron_at[0, :, stripe], (joint[at, stripe, :] * slope).astype(BF16))
+        total = term if begin == 0 else total + term
+        if step + 1 == len(ahead) or ahead[step + 1][0] != at:
+            unpair(d_agg, at, total)
 
     returning = []
     for number, piece in enumerate(BACK_PIECES):

time: 44.4 us -> 43.2 us (0.973)
  Pallas kernels: 43.5 us -> 42.3 us
    pallas_call x1, Pallas kernels: 42.4 us -> 41.2 us  [per_device(): pl.pallas_call(functools.partial(kernel, count_x, count_y), out_shape=(ja...]
where the time goes in v4:
time: 43.2 us; the launch traced here: 43.1 us
  Pallas kernels  42.3 us (98%)
  between operations  0.8 us (2%)
    pallas_call x1, Pallas kernels, per_device(): pl.pallas_call(functools.partial(kernel, count_x, count_y), out_shape=(ja...  41.2 us
    pallas_call x1, Pallas kernels, per_device(): pl.pallas_call(store_kernel, out_shape=(jax.ShapeDtypeStruct((ROWS, ATOMS...  1.05 us

profile of v4, /device:TPU:1, one launch (start us, length us, event | category | flops | bytes accessed | tf_op | source)
XLA Modules:
  0.0 43.1 jit_solution(15460546085138193707)
XLA Ops:
  0.6 41.2 %layer.1 = (bf16[1600,128]{1,0:T(8,128)(2,1)S(1)}, f32[1600,128]{1,0:T(8,128)S(1)}) custom-call(bf16[1600,128]{1,0:T(8,128)(2,1)} %bitcast.9, bf16[1600,128]{1,0:T(8,128)(2,1)} %bitcast.10, bf16[320,320]{1,0:T(8,128)(2,1)} %w0_hbm.1, bf16[2,256,256]{2,1,0:T(8,128)(2,1)} %w1_hbm.1, bf16[2,192,192]{2,1,0:T(8,128)(2,1)} %w2_hbm.1, bf16[2,128,128]{2,1,0:T(8,128)(2,1)} %w3_hbm.1, ...), custom_call_target="tpu_custom_call" | custom-call | tf_op jit(solution)/shard_map/layer/pallas_call | solution.py:442
  41.9 1.0 %store.1 = (bf16[1600,128]{1,0:T(8,128)(2,1)}, f32[1600,128]{1,0:T(8,128)}) custom-call(bf16[1600,128]{1,0:T(8,128)(2,1)S(1)} %get-tuple-element.6.layer_ref, f32[1600,128]{1,0:T(8,128)S(1)} %get-tuple-element.7.grad_ref), custom_call_target="tpu_custom_call" | custom-call | tf_op jit(solution)/shard_map/store/pallas_call | solution.py:519

commit v5 on v4

--- a/solution.py
+++ b/solution.py
@@ -297,8 +297,7 @@
             nn(kron[0, :, stripe], high) + nn(kron[1, :, stripe], high) + nn(kron[0, :, stripe], low)
         )
 
-    @pl.loop(0, 4)
-    def _(at):
+    for at in range(4):
         feat_pair = pair(feat32, at).astype(BF16)
         grid_feat[at] = nn(kron_a[0], feat_pair) + nn(kron_a[1], feat_pair)
         cot_pair = pair(cot32, at).astype(BF16)

time: 43.2 us -> 43.4 us (level)
  no operation moved by 1% of the time
where the time goes in v5:
time: 43.4 us; the launch traced here: 43 us
  Pallas kernels  42.2 us (97%)
  between operations  0.8 us (2%)
    pallas_call x1, Pallas kernels, per_device(): pl.pallas_call(functools.partial(kernel, count_x, count_y), out_shape=(ja...  41.2 us
    pallas_call x1, Pallas kernels, per_device(): pl.pallas_call(store_kernel, out_shape=(jax.ShapeDtypeStruct((ROWS, ATOMS...  1.05 us

profile of v5, /device:TPU:1, one launch (start us, length us, event | category | flops | bytes accessed | tf_op | source)
XLA Modules:
  0.0 43.0 jit_solution(3319477034987939759)
XLA Ops:
  0.6 41.2 %layer.1 = (bf16[1600,128]{1,0:T(8,128)(2,1)S(1)}, f32[1600,128]{1,0:T(8,128)S(1)}) custom-call(bf16[1600,128]{1,0:T(8,128)(2,1)} %bitcast.9, bf16[1600,128]{1,0:T(8,128)(2,1)} %bitcast.10, bf16[320,320]{1,0:T(8,128)(2,1)} %w0_hbm.1, bf16[2,256,256]{2,1,0:T(8,128)(2,1)} %w1_hbm.1, bf16[2,192,192]{2,1,0:T(8,128)(2,1)} %w2_hbm.1, bf16[2,128,128]{2,1,0:T(8,128)(2,1)} %w3_hbm.1, ...), custom_call_target="tpu_custom_call" | custom-call | tf_op jit(solution)/shard_map/layer/pallas_call | solution.py:441
  41.8 1.0 %store.1 = (bf16[1600,128]{1,0:T(8,128)(2,1)}, f32[1600,128]{1,0:T(8,128)}) custom-call(bf16[1600,128]{1,0:T(8,128)(2,1)S(1)} %get-tuple-element.6.layer_ref, f32[1600,128]{1,0:T(8,128)S(1)} %get-tuple-element.7.grad_ref), custom_call_target="tpu_custom_call" | custom-call | tf_op jit(solution)/shard_map/store/pallas_call | solution.py:518
